TPU v7x, 32 devices: a whole 2x2x4 slice. The times are simulated.
32 devices in a mesh: gx: 2 (over y), gy: 4 (over z), gz: 4 (over x, core).
Axes of the slice: x: 2, y: 2, z: 4, core: 2. Of those that a mesh axis runs over, the one named last changes fastest.
Arguments:
- moments: float32 [32, 128, 16, 128], P('gx', ('gy', 'gz')), may hold values from -128 to 128, as said below
- stiffness: float32 [32, 128, 16], P('gx', ('gy', 'gz')), may hold values from 0.5 to 4
- damping: float32 [32, 128, 16], P('gx', ('gy', 'gz')), may hold values from 0.05 to 1
- density: float32 [32, 128, 16], P('gx', ('gy', 'gz')), may hold values from 0.5 to 1.5
- ritz_coeffs: float32 [128, 128], replicated, may hold values from -128 to 128
- shifts: float32 [128], replicated, may hold values from -1.5 to -0.3
Outputs:
- ritz_vectors: float32 [32, 128, 16, 128], P('gx', ('gy', 'gz'))
- ritz_residual: float32 [32, 128, 16, 128], P('gx', ('gy', 'gz'))
- stiff_proj: float32 [128, 128], replicated
- damp_proj: float32 [128, 128], replicated
- mass_proj: float32 [128, 128], replicated
- first_factor: float32 [128, 128], replicated
Inputs may be any that keep to these rules, and one draw needn't show every extreme that they name: `moments`: A real block of full column rank.
All inputs are finite; a program needn't handle non-finite values.
Results may differ from a plain program's by a relative error of at most 0.0004.
Values sent between devices are 32-bit elements; how exact they have to be, the bound alone decides.
A program may use at most 64 MiB of HBM per device.

v0:
```python
import jax
import jax.numpy as jnp
from jax import lax
from jax.sharding import PartitionSpec as P


def with_halo(cells, sides, width):
    for axis, dim in sides:
        count = lax.axis_size(axis)
        ends = count - 1
        head = lax.slice_in_dim(cells, 0, width, axis=dim)
        tail = lax.slice_in_dim(cells, cells.shape[dim] - width, cells.shape[dim], axis=dim)
        cells = jnp.concatenate(
            [
                lax.ppermute(tail, axis, [(i, (i + 1) % count) for i in range(ends)]),
                cells,
                lax.ppermute(head, axis, [((i + 1) % count, i) for i in range(ends)]),
            ],
            axis=dim,
        )
    return cells


def factorize(gram):
    count = gram.shape[0]
    index = jnp.arange(count, dtype=jnp.int32)

    def column_step(j, carry):
        work, lower = carry
        onehot = (index == j).astype(gram.dtype)
        column = jnp.sum(work * onehot[None, :], axis=1)
        pivot = jnp.sum(column * onehot)
        column = jnp.where(index >= j, column, jnp.zeros_like(column)) / jnp.sqrt(pivot)
        lower = lower + column[:, None] * onehot[None, :]
        work = work - column[:, None] * column[None, :]
        return (work, lower)

    start = (gram, jnp.zeros_like(gram))
    lower = lax.fori_loop(0, count, column_step, start)[1]

    def row_step(i, inverse):
        onehot = (index == i).astype(gram.dtype)
        row = jnp.sum(lower * onehot[:, None], axis=0)
        pivot = jnp.sum(row * onehot)
        rhs = onehot - jnp.sum(row[:, None] * inverse, axis=0)
        return inverse + onehot[:, None] * (rhs / pivot)[None, :]

    inverse = lax.fori_loop(0, count, row_step, jnp.zeros_like(gram))
    return (lower, inverse.T)


def matmul(left, right):
    return jnp.dot(left, right, precision=lax.Precision.HIGHEST)


def apply_stencils(flat, shape, stiff_col, dens_col):
    field = flat.reshape(shape)
    padded = with_halo(field, (("gx", 0), (("gy", "gz"), 1)), 1)
    near = padded[2:, 1:-1] + padded[:-2, 1:-1]
    near = near + padded[1:-1, 2:] + padded[1:-1, :-2]
    plane = jnp.zeros((shape[0], shape[1], 1, shape[3]), jnp.float32)
    near = near + jnp.concatenate([field[:, :, 1:], plane], axis=2)
    near = near + jnp.concatenate([plane, field[:, :, :-1]], axis=2)
    near = near.reshape(flat.shape)
    return ((6.0 + stiff_col) * flat - near, dens_col * flat + near / 12.0)


def local(moments, stiffness, damping, density, ritz_coeffs, shifts):
    shape = moments.shape
    cells = shape[0] * shape[1] * shape[2]
    width = shape[3]
    all_cells = cells * lax.axis_size("gx") * lax.axis_size("gy") * lax.axis_size("gz")
    flat = moments.reshape(cells, width)
    stiff_col = stiffness.reshape(cells, 1)
    damp_col = damping.reshape(cells, 1)
    dens_col = density.reshape(cells, 1)
    lower_one, first_inv = factorize(lax.psum(matmul(flat.T, flat), ("gx", "gy", "gz")))
    first_factor = lower_one.T / jnp.sqrt(jnp.float32(all_cells))
    basis_one = matmul(flat, first_inv)
    k_block, m_block = apply_stencils(basis_one, shape, stiff_col, dens_col)
    c_block = damp_col * basis_one
    gram_two, stiff_one, damp_one, mass_one = lax.psum(
        (
            matmul(basis_one.T, basis_one),
            matmul(basis_one.T, k_block),
            matmul(basis_one.T, c_block),
            matmul(basis_one.T, m_block),
        ),
        ("gx", "gy", "gz"),
    )
    second_inv = factorize(gram_two)[1]
    stiff_proj = matmul(second_inv.T, matmul(stiff_one, second_inv))
    damp_proj = matmul(second_inv.T, matmul(damp_one, second_inv))
    mass_proj = matmul(second_inv.T, matmul(mass_one, second_inv))
    coeffs = matmul(second_inv, ritz_coeffs)
    ritz = matmul(basis_one, coeffs)
    resid = matmul(k_block, coeffs)
    resid = resid + matmul(c_block, coeffs) * shifts
    resid = resid + matmul(m_block, coeffs) * (shifts * shifts)
    return (
        ritz.reshape(shape),
        resid.reshape(shape),
        stiff_proj,
        damp_proj,
        mass_proj,
        first_factor,
    )


def solution(mesh):
    return jax.shard_map(
        local,
        mesh=mesh,
        in_specs=(
            P("gx", ("gy", "gz"), None, None),
            P("gx", ("gy", "gz"), None),
            P("gx", ("gy", "gz"), None),
            P("gx", ("gy", "gz"), None),
            P(),
            P(),
        ),
        out_specs=(
            P("gx", ("gy", "gz"), None, None),
            P("gx", ("gy", "gz"), None, None),
            P(),
            P(),
            P(),
            P(),
        ),
        check_vma=False,
    )
```

profile of v0, /device:TPU:0, one launch (start us, length us, event | category | flops | bytes accessed | tf_op | source)
XLA Modules:
  0.0 1594.6 jit_solution(11436615384494239305)
XLA Ops:
  8.4 2.5 convolution_bitcast_fusion
  13.7 120.7 %all-reduce.6.cloned.1.call-done = f32[128,128]{1,0:T(8,128)} async-done(((f32[128,128]{1,0:T(8,128)}), f32[128,128]{1,0:T(8,128)}) %all-reduce.6.cloned.1.call-update) | async-done | bytes 65552 | tf_op jit(solution)/shard_map/psum | solution.py:77
  134.5 488.4 %while.64 = (s32[]{:T(128)}, f32[128,128]{1,0:T(8,128)}, f32[128,128]{1,0:T(8,128)S(1)}, s32[]{:T(128)}, s32[]{:T(128)}) while((s32[]{:T(128)}, f32[128,128]{1,0:T(8,128)}, f32[128,128]{1,0:T(8,128)S(1)}, s32[]{:T(128)}, s32[]{:T(128)}) %tuple.132), condition=%wide.region_4.5_spmd.clone.clone, body=%wide.region_1.4_spmd.clone.clone.sunk | while | flops 115586 | bytes 331875 | solution.py:39
  136.7 1.5 select_add_fusion.4
  144.4 1.5 select_add_fusion.4
  152.0 1.5 select_add_fusion.4
  159.6 1.5 select_add_fusion.4
  167.3 1.5 select_add_fusion.4
  171.1 1.5 select_add_fusion.4
  178.7 1.5 select_add_fusion.4
  186.3 1.5 select_add_fusion.4
  194.0 1.5 select_add_fusion.4
  201.6 1.5 select_add_fusion.4
  209.2 1.5 select_add_fusion.4
  216.9 1.5 select_add_fusion.4
  224.5 1.5 select_add_fusion.4
  232.1 1.5 select_add_fusion.4
  239.8 1.5 select_add_fusion.4
  243.6 1.5 select_add_fusion.4
  251.2 1.5 select_add_fusion.4
  258.8 1.5 select_add_fusion.4
  266.5 1.5 select_add_fusion.4
  274.1 1.5 select_add_fusion.4
  281.7 1.5 select_add_fusion.4
  289.4 1.5 select_add_fusion.4
  297.0 1.5 select_add_fusion.4
  304.6 1.5 select_add_fusion.4
  312.3 1.5 select_add_fusion.4
  316.1 1.5 select_add_fusion.4
  323.7 1.5 select_add_fusion.4
  331.3 1.5 select_add_fusion.4
  339.0 1.5 select_add_fusion.4
  622.9 202.8 %while.62 = (s32[]{:T(128)}, f32[128,128]{1,0:T(8,128)S(1)}, f32[128,128]{1,0:T(8,128)S(1)}, s32[]{:T(128)}, s32[]{:T(128)}) while((s32[]{:T(128)}, f32[128,128]{1,0:T(8,128)S(1)}, f32[128,128]{1,0:T(8,128)S(1)}, s32[]{:T(128)}, s32[]{:T(128)}) %tuple.135), condition=%wide.region_9.10_spmd.clone, body=%wide.region_5.9_spmd.clone.sunk | while | flops 131970 | bytes 267356 | solution.py:48
  829.8 4.5 collective-permute-start.1
  834.3 1.6 fusion.39
  835.9 1.7 fusion.21
  839.0 3.9 collective-permute-start.3
  842.9 1.6 fusion.42
  845.8 1.6 copy.18
  847.4 1.7 fusion.28
  849.1 1.7 fusion.26
  851.5 127.3 %all-reduce.8.cloned.1.call-done = (f32[128,128]{1,0:T(8,128)}, f32[128,128]{1,0:T(8,128)}, f32[128,128]{1,0:T(8,128)}, f32[128,128]{1,0:T(8,128)}) async-done(((f32[128,128]{1,0:T(8,128)}, f32[128,128]{1,0:T(8,128)}, f32[128,128]{1,0:T(8,128)}, f32[128,128]{1,0:T(8,128)}), (f32[128,128]{1,0:T(8,128)}, f32[128,128]{1,0:T(8,128)}, f32[128,128]{1,0:T(8,128)}, ...) | async-done | bytes 262160 | tf_op jit(solution)/shard_map/psum | solution.py:82
  978.8 393.4 %while.65 = (s32[]{:T(128)}, f32[128,128]{1,0:T(8,128)}, f32[128,128]{1,0:T(8,128)S(1)}, s32[]{:T(128)}, s32[]{:T(128)}) while((s32[]{:T(128)}, f32[128,128]{1,0:T(8,128)}, f32[128,128]{1,0:T(8,128)S(1)}, s32[]{:T(128)}, s32[]{:T(128)}) %tuple.138), condition=%wide.region_14.15_spmd.clone.clone, body=%wide.region_11.14_spmd.clone.clone.sunk | while | flops 115586 | bytes 856219 | solution.py:39
  1372.2 202.7 %while.63 = (s32[]{:T(128)}, f32[128,128]{1,0:T(8,128)S(1)}, f32[128,128]{1,0:T(8,128)S(1)}, s32[]{:T(128)}, s32[]{:T(128)}) while((s32[]{:T(128)}, f32[128,128]{1,0:T(8,128)S(1)}, f32[128,128]{1,0:T(8,128)S(1)}, s32[]{:T(128)}, s32[]{:T(128)}) %tuple.141), condition=%wide.region_19.0_spmd.clone, body=%wide.region_15.19_spmd.clone.sunk | while | flops 131970 | bytes 267356 | solution.py:48
  1575.2 1.8 fusion.27
  1577.0 2.8 fusion.44
  1583.2 1.8 fusion.15
  1585.0 2.8 fusion.14
  (3362 shorter events, 1060.6 us)
Async XLA Ops:
  7.2 127.3 %all-reduce.6.cloned.1.call-start = ((), (), s32[]{:S(2)}) async-start(), calls=%async_computation | async-start | bytes 131072 | tf_op jit(solution)/shard_map/psum | solution.py:77
  10.9 967.9 %all-reduce.8.cloned.1.call-start = ((), (), s32[]{:S(2)}) async-start(), calls=%async_computation.1 | async-start | bytes 524288 | tf_op jit(solution)/shard_map/psum | solution.py:82
  827.8 9.9 collective-permute-start
  829.8 7.9 collective-permute-start.1
  837.7 6.8 collective-permute-start.2
  839.0 5.5 copy-start.3
  839.0 5.5 copy-start.4
  839.0 5.5 collective-permute-start.3
  984.9 2.3 copy-start.1
  988.0 2.3 copy-start.1
  991.1 2.3 copy-start.1
  1000.3 2.3 copy-start.1
  1003.4 2.3 copy-start.1
  1006.4 2.3 copy-start.1
  1015.7 2.3 copy-start.1
  1018.7 2.3 copy-start.1
  1028.0 2.3 copy-start.1
  1031.0 2.3 copy-start.1
  1034.1 2.3 copy-start.1
  1043.3 2.3 copy-start.1
  1046.4 2.3 copy-start.1
  1049.5 2.3 copy-start.1
  1058.7 2.3 copy-start.1
  1061.8 2.3 copy-start.1
  1064.8 2.3 copy-start.1
  1074.1 2.3 copy-start.1
  1077.1 2.3 copy-start.1
  1086.4 2.3 copy-start.1
  1089.4 2.3 copy-start.1
  1092.5 2.3 copy-start.1
  1101.7 2.3 copy-start.1
  1104.8 2.3 copy-start.1
  1107.9 2.3 copy-start.1
  1117.1 2.3 copy-start.1
  1120.2 2.3 copy-start.1
  1123.2 2.3 copy-start.1
  1132.5 2.3 copy-start.1
  1135.5 2.3 copy-start.1
  1144.8 2.3 copy-start.1
  1147.8 2.3 copy-start.1
  1150.9 2.3 copy-start.1
  1160.1 2.3 copy-start.1
  1163.2 2.3 copy-start.1
  1166.3 2.3 copy-start.1
  1175.5 2.3 copy-start.1
  1178.6 2.3 copy-start.1
  1372.2 202.7 %copy-start.6 = (f32[128,128]{1,0:T(8,128)S(1)}, f32[128,128]{1,0:T(8,128)}, u32[]{:S(2)}) copy-start(f32[128,128]{1,0:T(8,128)} %param.18) | copy-start | bytes 196612
  1577.0 2.8 copy-start.9
  (228 other events, 301.2 us)
Sparse Core Ops, SparseCore 0:
  14.2 120.2 all-reduce.5
  850.9 127.7 all-reduce.7
where the time goes:
time: 1620 us; the launch traced here: 1590 us
  other arithmetic  1010 us (62%)
  waiting for transfers between devices  248 us (15%)
  loops' own time  197 us (12%)
  local copies, waits for them, and re-layouts  87.3 us (5%)
  matrix products  22.9 us (1%)
    reduce_sum x256, other arithmetic, column_step(): column = jnp.sum(work * onehot[None, :], axis=1)  249 us
    add x256, other arithmetic, column_step(): lower = lower + column[:, None] * onehot[None, :]  209 us
    another operation x2, loops' own time, factorize(): lower = lax.fori_loop(0, count, column_step, start)[1]  186 us
    div x256, other arithmetic, row_step(): return inverse + onehot[:, None] * (rhs / pivot)[None, :]  166 us
    reduce_sum x256, other arithmetic, column_step(): pivot = jnp.sum(column * onehot)  157 us
    reduce_sum x256, other arithmetic, row_step(): pivot = jnp.sum(row * onehot)  155 us
    psum x1, waiting for transfers between devices, local(): lax.psum((matmul(basis_one.T, basis_one), matmul(basis_one.T, k_block), m...  127 us
    psum x1, waiting for transfers between devices, local(): lax.psum(matmul(flat.T, flat), ('gx', 'gy', 'gz'))  121 us
  transfers between devices with their start and end apart: 6, of which 2 were waited for; matrix products, arithmetic and copies ran while one was open for 0% of the time, Pallas kernels for 0%

commit v1 on v0

v1 whole, which is shorter than its diff:
```python
import functools
import math
import jax
import jax.numpy as jnp
from jax import lax
from jax.experimental import pallas as pl
from jax.experimental.pallas import tpu as pltpu
from jax.sharding import PartitionSpec as P

MESH = pl.DeviceIdType.MESH
HI = lax.Precision.HIGHEST
F32 = jnp.float32
BLK = 8


def mm(a, b):
    return lax.dot_general(a, b, (((1,), (0,)), ((), ())), precision=HI, preferred_element_type=F32)


def mm_t(a, b):
    return lax.dot_general(a, b, (((0,), (0,)), ((), ())), precision=HI, preferred_element_type=F32)


def factorize(work, upper, inverse):
    n = work.shape[0]
    lane = lax.broadcasted_iota(jnp.int32, (BLK, n), 1)
    sub = lax.broadcasted_iota(jnp.int32, (BLK, n), 0)
    lane_all = lax.broadcasted_iota(jnp.int32, (n, n), 1)

    def block(jb, carry):
        first = pl.multiple_of(jb * BLK, BLK)
        rows = work[pl.ds(first, BLK), :]
        cols = [
            jnp.broadcast_to(
                jnp.sum(jnp.where(lane == first + k, rows, 0.0), axis=1, keepdims=True), (BLK, n)
            )
            for k in range(BLK)
        ]
        u = jnp.where(lane >= first, rows, 0.0)
        e = jnp.where(lane < first, rows, jnp.where(lane == first + sub, 1.0, 0.0))
        pivots = jnp.zeros((BLK, n), F32)
        for s in range(BLK):
            pivot = jnp.broadcast_to(cols[s][s : s + 1], (BLK, n))
            pivots = jnp.where(sub == s, pivot, pivots)
            if s == BLK - 1:
                break
            m = jnp.where(sub > s, cols[s] / pivot, 0.0)
            for k in range(s + 1, BLK):
                cols[k] = cols[k] - m * cols[k][s : s + 1]
            u = u - m * u[s : s + 1]
            e = e - m * e[s : s + 1]
        scale = 1.0 / jnp.sqrt(pivots)
        u = jnp.where(lane >= first + sub, u * scale, 0.0)
        e = e * scale
        upper[pl.ds(first, BLK), :] = u
        inverse[pl.ds(first, BLK), :] = e
        beyond = jnp.where(lane >= first + BLK, u, 0.0)
        panel = (lane_all >= first) & (lane_all < first + BLK)
        work[...] = jnp.where(panel, 0.0, work[...]) - mm_t(beyond, beyond + e)
        return carry

    lax.fori_loop(0, n // BLK, block, 0)


def kernel(
    sizes,
    y_ref, fields_ref, ritz_ref, shifts_ref,
    vec_ref, res_ref, stiff_ref, damp_ref, mass_ref, factor_ref,
    pad, halo_x, halo_y, work, upper, inv_a, inv_b,
    g_src, g_recv, g_z, g_full, h_recv, h_z, h_full, p_src, p_recv, p_z, p_full, h_src, proj,
    halo_send, halo_got, a_send, a_got, z_send, z_got, b_send, b_got,
):
    nx, ny, nz, all_cells = sizes
    bx, by, bz, w = y_ref.shape
    group = nx * nz
    ix, iy, iz = lax.axis_index("gx"), lax.axis_index("gy"), lax.axis_index("gz")
    mine = ix * nz + iz
    line = iy * nz + iz

    def group_id(a):
        return (lax.div(a, nz), iy, lax.rem(a, nz))

    def line_id(a):
        return (ix, lax.div(a, nz), lax.rem(a, nz))

    sides = [
        (ix > 0, (ix - 1, iy, iz), y_ref.at[0], halo_x.at[1], halo_x.at[0]),
        (ix < nx - 1, (ix + 1, iy, iz), y_ref.at[bx - 1], halo_x.at[0], halo_x.at[1]),
        (line > 0, line_id(line - 1), y_ref.at[:, 0], halo_y.at[1], halo_y.at[0]),
        (line < ny * nz - 1, line_id(line + 1), y_ref.at[:, by - 1], halo_y.at[0], halo_y.at[1]),
    ]
    peers = [lax.rem(mine + d, group) for d in range(1, group)]
    planes = [lax.rem(iy + d, ny) for d in range(1, ny)]

    barrier = pltpu.get_barrier_semaphore()
    for peer in peers:
        pl.semaphore_signal(barrier, inc=1, device_id=group_id(peer), device_id_type=MESH)
    for plane in planes:
        pl.semaphore_signal(barrier, inc=1, device_id=(ix, plane, iz), device_id_type=MESH)
    for exists, device, _, _, _ in sides:
        @pl.when(exists)
        def _():
            pl.semaphore_signal(barrier, inc=1, device_id=device, device_id_type=MESH)

    def gram_step(i, total):
        rows = y_ref[pl.ds(i * 4, 4)].reshape(4 * by * bz, w)
        return total + mm_t(rows, rows)

    work[...] = lax.fori_loop(0, bx // 4, gram_step, jnp.zeros((w, w), F32))

    beside = sum(exists.astype(jnp.int32) for exists, _, _, _, _ in sides)
    pl.semaphore_wait(barrier, group - 1 + ny - 1 + beside)

    def halo_copy(k):
        _, device, src, dst, _ = sides[k]
        other = k ^ 1
        return pltpu.make_async_remote_copy(
            src_ref=src, dst_ref=dst, send_sem=halo_send.at[k], recv_sem=halo_got.at[other],
            device_id=device, device_id_type=MESH,
        )

    def scatter_start(slot, src, recv):
        copies = []
        for d, peer in enumerate(peers):
            copy = pltpu.make_async_remote_copy(
                src_ref=src.at[peer], dst_ref=recv.at[d], send_sem=a_send.at[slot, d],
                recv_sem=a_got.at[slot, d], device_id=group_id(peer), device_id_type=MESH,
            )
            copy.start()
            copies.append(copy)
        return copies

    def plane_start(slot, copies, src, recv, z):
        for copy in copies:
            copy.wait_recv()
        total = src[mine]
        for d in range(group - 1):
            total = total + recv[d]
        z[iy] = total
        after = []
        for d, plane in enumerate(planes):
            copy = pltpu.make_async_remote_copy(
                src_ref=z.at[iy], dst_ref=z.at[iy], send_sem=z_send.at[slot, d],
                recv_sem=z_got.at[slot, d], device_id=(ix, plane, iz), device_id_type=MESH,
            )
            copy.start()
            after.append(copy)
        return after

    def gather_start(slot, copies, z, full):
        for copy in copies:
            copy.wait_recv()
        total = z[0]
        for d in range(1, ny):
            total = total + z[d]
        full[mine] = total
        after = []
        for d, peer in enumerate(peers):
            copy = pltpu.make_async_remote_copy(
                src_ref=full.at[mine], dst_ref=full.at[mine], send_sem=b_send.at[slot, d],
                recv_sem=b_got.at[slot, d], device_id=group_id(peer), device_id_type=MESH,
            )
            copy.start()
            after.append(copy)
        return after

    def gather_end(copies, full, out):
        for copy in copies:
            copy.wait_recv()
        r = full.shape[1]
        for a in range(group):
            out[a * r : (a + 1) * r, :] = full[a]

    def chunks(src, out):
        r = out.shape[1]
        for a in range(group):
            out[a] = src[a * r : (a + 1) * r, :]

    chunks(work, g_src)
    s1 = scatter_start(0, g_src, g_recv)
    for k, (exists, _, _, _, land) in enumerate(sides):
        @pl.when(exists)
        def _():
            halo_copy(k).start()

        @pl.when(jnp.logical_not(exists))
        def _():
            land[...] = jnp.zeros(land.shape, F32)
    s2 = plane_start(0, s1, g_src, g_recv, g_z)
    s3 = gather_start(0, s2, g_z, g_full)
    gather_end(s3, g_full, work)
    factorize(work, upper, inv_a)
    factor_ref[...] = upper[...] / math.sqrt(all_cells)

    for k, (exists, _, _, _, _) in enumerate(sides):
        @pl.when(exists)
        def _():
            halo_copy(k).wait_send()
            halo_copy(k ^ 1).wait_recv()
    first_inv = inv_a[...].T

    def basis_step(i, carry):
        rows = y_ref[pl.ds(i * 4, 4)].reshape(4 * by * bz, w)
        pad[pl.ds(i * 4 + 1, 4), 1 : by + 1] = mm(rows, first_inv).reshape(4, by, bz, w)
        return carry

    lax.fori_loop(0, bx // 4, basis_step, 0)
    for side, at in ((0, 0), (1, bx + 1)):
        pad[at, 1 : by + 1] = mm(halo_x[side].reshape(by * bz, w), first_inv).reshape(by, bz, w)
    for side, at in ((0, 0), (1, by + 1)):
        pad[1 : bx + 1, at] = mm(halo_y[side].reshape(bx * bz, w), first_inv).reshape(bx, bz, w)

    zero = jnp.zeros((by, 1, w), F32)

    def near_of(x):
        q = pad[x + 1, 1 : by + 1]
        near = pad[x, 1 : by + 1] + pad[x + 2, 1 : by + 1]
        near = near + pad[x + 1, 0:by] + pad[x + 1, 2 : by + 2]
        near = near + jnp.concatenate([q[:, 1:], zero], axis=1)
        near = near + jnp.concatenate([zero, q[:, :-1]], axis=1)
        return q, near

    def field(f, x):
        cell = fields_ref[f, x]
        return jnp.stack([jnp.broadcast_to(cell[:, y : y + 1], (bz, w)) for y in range(by)])

    def flat(v):
        return v.reshape(by * bz, w)

    def gram_two_step(i, total):
        rows = pad[pl.ds(i * 4 + 1, 4), 1 : by + 1].reshape(4 * by * bz, w)
        return total + mm_t(rows, rows)

    h = lax.fori_loop(0, bx // 4, gram_two_step, jnp.zeros((w, w), F32))
    work[...] = h
    chunks(work, h_src)
    t1 = scatter_start(1, h_src, h_recv)

    proj[...] = jnp.zeros(proj.shape, F32)

    def proj_step(x, carry):
        q, near = near_of(x)
        k_block = (6.0 + field(0, x)) * q - near
        c_block = field(1, x) * q
        m_block = field(2, x) * q + near * (1.0 / 12.0)
        wide = jnp.concatenate([flat(k_block), flat(c_block), flat(m_block)], axis=1)
        out = mm_t(flat(q), wide)
        for p in range(3):
            proj[p * w : (p + 1) * w, :] += out[:, p * w : (p + 1) * w]
        return carry

    lax.fori_loop(0, bx, proj_step, 0)
    chunks(proj, p_src)
    r1 = scatter_start(2, p_src, p_recv)
    t2 = plane_start(1, t1, h_src, h_recv, h_z)
    t3 = gather_start(1, t2, h_z, h_full)
    r2 = plane_start(2, r1, p_src, p_recv, p_z)
    gather_end(t3, h_full, work)
    factorize(work, upper, inv_b)
    r3 = gather_start(2, r2, p_z, p_full)

    left = inv_b[...]
    second_inv = left.T
    coeffs = mm(second_inv, ritz_ref[...])

    def vector_step(i, carry):
        rows = pad[pl.ds(i * 2, 2)].reshape(2 * (by + 2) * bz, w)
        pad[pl.ds(i * 2, 2)] = mm(rows, coeffs).reshape(2, by + 2, bz, w)
        return carry

    pad[0, 0] = jnp.zeros((bz, w), F32)
    pad[0, by + 1] = jnp.zeros((bz, w), F32)
    pad[bx + 1, 0] = jnp.zeros((bz, w), F32)
    pad[bx + 1, by + 1] = jnp.zeros((bz, w), F32)
    lax.fori_loop(0, (bx + 2) // 2, vector_step, 0)
    shifts = shifts_ref[...].reshape(1, 1, w)
    squares = shifts * shifts

    def residual_step(x, carry):
        v, near = near_of(x)
        vec_ref[x] = v
        stiff = (6.0 + field(0, x)) * v - near
        res_ref[x] = stiff + field(1, x) * v * shifts + (field(2, x) * v + near * (1.0 / 12.0)) * squares
        return carry

    lax.fori_loop(0, bx, residual_step, 0)

    gather_end(r3, p_full, proj)
    for p, out in enumerate((stiff_ref, damp_ref, mass_ref)):
        out[...] = mm(left, mm(proj[p * w : (p + 1) * w, :], second_inv))
    for copies in (s1, s2, s3, t1, t2, t3, r1, r2, r3):
        for copy in copies:
            copy.wait_send()


def local(sizes, moments, stiffness, damping, density, ritz_coeffs, shifts):
    nx, ny, nz, _ = sizes
    bx, by, bz, w = moments.shape
    group = nx * nz
    fields = jnp.stack([stiffness, damping, density]).transpose(0, 1, 3, 2)
    r = w // group
    q = 3 * w // group
    mat = jax.ShapeDtypeStruct((w, w), F32)
    block = jax.ShapeDtypeStruct(moments.shape, F32)
    square = pltpu.VMEM((w, w), F32)
    vmem = pl.BlockSpec(memory_space=pltpu.VMEM)
    dma = pltpu.SemaphoreType.DMA
    return pl.pallas_call(
        functools.partial(kernel, sizes),
        out_shape=(block, block, mat, mat, mat, mat),
        in_specs=[vmem] * 4,
        out_specs=(vmem,) * 6,
        scratch_shapes=[
            pltpu.VMEM((bx + 2, by + 2, bz, w), F32),
            pltpu.VMEM((2, by, bz, w), F32),
            pltpu.VMEM((2, bx, bz, w), F32),
            square, square, square, square,
            pltpu.VMEM((group, r, w), F32),
            pltpu.VMEM((group, r, w), F32),
            pltpu.VMEM((ny, r, w), F32),
            pltpu.VMEM((group, r, w), F32),
            pltpu.VMEM((group, r, w), F32),
            pltpu.VMEM((ny, r, w), F32),
            pltpu.VMEM((group, r, w), F32),
            pltpu.VMEM((group, q, w), F32),
            pltpu.VMEM((group, q, w), F32),
            pltpu.VMEM((ny, q, w), F32),
            pltpu.VMEM((group, q, w), F32),
            pltpu.VMEM((group, r, w), F32),
            pltpu.VMEM((3 * w, w), F32),
            dma((4,)), dma((4,)),
            dma((3, group - 1)), dma((3, group - 1)),
            dma((3, ny - 1)), dma((3, ny - 1)),
            dma((3, group - 1)), dma((3, group - 1)),
        ],
        compiler_params=pltpu.CompilerParams(
            collective_id=0, has_side_effects=True, vmem_limit_bytes=48 << 20
        ),
    )(moments, fields, ritz_coeffs, shifts.reshape(1, w))


def solution(mesh):
    nx, ny, nz = (mesh.shape[a] for a in ("gx", "gy", "gz"))

    def call(moments, *rest):
        cells = moments.shape[0] * moments.shape[1] * moments.shape[2]
        body = functools.partial(local, (nx, ny, nz, cells * nx * ny * nz))
        return body(moments, *rest)

    cube = P("gx", ("gy", "gz"), None)
    block = P("gx", ("gy", "gz"), None, None)
    return jax.shard_map(
        call,
        mesh=mesh,
        in_specs=(block, cube, cube, cube, P(), P()),
        out_specs=(block, block, P(), P(), P(), P()),
        check_vma=False,
    )
```

time: 1620 us -> 64.5 us (0.04); the launches traced: 1590 us -> 64.2 us
  other arithmetic: 1010 us -> 0.03 us
  waiting for transfers between devices: 248 us -> 0 us
  loops' own time: 197 us -> 0 us
  local copies, waits for them, and re-layouts: 87.3 us -> 8.12 us
  Pallas kernels: 0 us -> 55.3 us
  matrix products: 22.9 us -> 0 us
    reduce_sum x1280 -> x0, other arithmetic: 611 us -> none  [the longest x256 249 us: column_step(): column = jnp.sum(work * onehot[None, :], axis=1)]
    psum x2 -> x0, waiting for transfers between devices: 248 us -> none  [the longest x1 127 us: local(): lax.psum((matmul(basis_one.T, basis_one), matmul(basis_one.T, k_block), m...]
    add x514 -> x0, other arithmetic: 232 us -> none  [the longest x256 209 us: column_step(): lower = lower + column[:, None] * onehot[None, :]]
    another operation x4 -> x0, loops' own time: 197 us -> none  [the longest x2 186 us: factorize(): lower = lax.fori_loop(0, count, column_step, start)[1]]
    div x513 -> x0, other arithmetic: 168 us -> none  [the longest x256 166 us: row_step(): return inverse + onehot[:, None] * (rhs / pivot)[None, :]]
    while x513 -> x0, local copies, waits for them, and re-layouts: 78.9 us -> none
    pallas_call x0 -> x1, Pallas kernels: none -> 55.3 us  [local(): pl.pallas_call(functools.partial(kernel, sizes), out_shape=(block, block,...]
    dot_general x17 -> x0, matrix products: 22.9 us -> none  [matmul(): return jnp.dot(left, right, precision=lax.Precision.HIGHEST)]
  transfers between devices with their start and end apart: 6 -> 0, of which waited for: 2 -> 0; matrix products, arithmetic and copies ran while one was open for 0% -> 0% of each run, Pallas kernels for 0% -> 0%
where the time goes in v1:
time: 64.5 us; the launch traced here: 64.2 us
  Pallas kernels  55.3 us (86%)
  local copies, waits for them, and re-layouts  8.12 us (13%)
  between operations  0.71 us (1%)
    pallas_call x1, Pallas kernels, local(): pl.pallas_call(functools.partial(kernel, sizes), out_shape=(block, block,...  55.3 us
    unnamed x15, local copies, waits for them, and re-layouts  8.12 us

profile of v1, /device:TPU:0, one launch (start us, length us, event | category | flops | bytes accessed | tf_op | source)
XLA Modules:
  0.0 64.2 jit_solution(15921971637814061802)
XLA Ops:
  0.6 0.0 copy-start
  0.6 1.0 %copy.12 = f32[16,8,16]{1,2,0:T(8,128)S(1)} copy(f32[16,8,16]{2,1,0:T(8,128)} %param.7) | data formatting | bytes 16384 | tf_op args[1]
  1.7 0.9 %copy.13 = f32[16,8,16]{1,2,0:T(8,128)S(1)} copy(f32[16,8,16]{2,1,0:T(8,128)} %param.8) | data formatting | bytes 16384 | tf_op args[2]
  2.6 0.9 %copy.14 = f32[16,8,16]{1,2,0:T(8,128)S(1)} copy(f32[16,8,16]{2,1,0:T(8,128)} %param.9) | data formatting | bytes 16384 | tf_op args[3]
  3.5 0.0 copy-start.1
  3.6 0.0 copy-start.2
  3.6 0.0 copy-done
  3.6 0.8 %copy-done.1 = f32[128,128]{1,0:T(8,128)S(1)} copy-done((f32[128,128]{1,0:T(8,128)S(1)}, f32[128,128]{1,0:T(8,128)}, u32[]{:S(2)}) %copy-start.1) | copy-done | bytes 65560
  4.4 0.0 copy-done.2
  4.4 55.3 %shard_map.109 = (f32[16,8,16,128]{3,2,1,0:T(8,128)S(1)}, f32[16,8,16,128]{3,2,1,0:T(8,128)S(1)}, f32[128,128]{1,0:T(8,128)S(1)}, f32[128,128]{1,0:T(8,128)S(1)}...) custom-call(f32[16,8,16,128]{3,2,1,0:T(8,128)S(1)} %copy-done, f32[3,16,16,8]{3,2,1,0:T(8,128)S(1)} %maximum_bitcast_fusion.fields_ref, ...), custom_call_target="tpu_custom_call" | custom-call | tf_op jit(solution)/shard_map/pallas_call | solution.py:308
  59.7 1.0 %copy.21 = f32[16,8,16,128]{3,2,1,0:T(8,128)} copy(f32[16,8,16,128]{3,2,1,0:T(8,128)S(1)} %get-tuple-element.12) | data formatting | bytes 2097152
  60.7 1.0 %copy.22 = f32[16,8,16,128]{3,2,1,0:T(8,128)} copy(f32[16,8,16,128]{3,2,1,0:T(8,128)S(1)} %get-tuple-element.13) | data formatting | bytes 2097152
  61.7 0.6 copy.23
  62.3 0.6 copy.24
  62.9 0.6 copy.25
  63.6 0.6 copy.26
  (1 shorter events, 0.0 us)
Async XLA Ops:
  0.6 3.0 %copy-start = (f32[16,8,16,128]{3,2,1,0:T(8,128)S(1)}, f32[16,8,16,128]{3,2,1,0:T(8,128)}, u32[]{:S(2)}) copy-start(f32[16,8,16,128]{3,2,1,0:T(8,128)} %y_ref.1) | copy-start | bytes 3145732
  3.5 0.8 %copy-start.1 = (f32[128,128]{1,0:T(8,128)S(1)}, f32[128,128]{1,0:T(8,128)}, u32[]{:S(2)}) copy-start(f32[128,128]{1,0:T(8,128)} %ritz_ref.1) | copy-start | bytes 196612
  3.6 0.8 %copy-start.2 = (f32[128]{0:T(128)S(1)}, f32[128]{0:T(128)}, u32[]{:S(2)}) copy-start(f32[128]{0:T(128)} %param.11) | copy-start | bytes 1540

commit v2 on v1

--- a/solution.py
+++ b/solution.py
@@ -10,7 +10,8 @@
 MESH = pl.DeviceIdType.MESH
 HI = lax.Precision.HIGHEST
 F32 = jnp.float32
-BLK = 8
+BF16 = jnp.bfloat16
+BLK = 16
 
 
 def mm(a, b):
@@ -19,6 +20,75 @@
 
 def mm_t(a, b):
     return lax.dot_general(a, b, (((0,), (0,)), ((), ())), precision=HI, preferred_element_type=F32)
+
+
+def split(x):
+    high = x.astype(BF16)
+    return high, (x - high.astype(F32)).astype(BF16)
+
+
+def split3(x):
+    high = x.astype(BF16)
+    rest = x - high.astype(F32)
+    mid = rest.astype(BF16)
+    return high, mid, (rest - mid.astype(F32)).astype(BF16)
+
+
+def dot_t(a, b):
+    return lax.dot_general(a, b, (((0,), (0,)), ((), ())), preferred_element_type=F32)
+
+
+def dot(a, b):
+    return lax.dot_general(a, b, (((1,), (0,)), ((), ())), preferred_element_type=F32)
+
+
+def rank_update(a, b):
+    ah, am, al = split3(a)
+    bh, bm, bl = split3(b)
+    left = jnp.concatenate([ah, am, ah, am, ah, al], axis=0)
+    right = jnp.concatenate([bh, bh, bm, bm, bl, bh], axis=0)
+    return dot_t(left, right)
+
+
+def coeff_tile(c):
+    high, low = split(c)
+    return jnp.concatenate(
+        [jnp.concatenate([high, low], axis=1), jnp.concatenate([high, jnp.zeros_like(high)], axis=1)], axis=0
+    )
+
+
+def mm_three(rows, tile):
+    w = rows.shape[1]
+    out = dot(jnp.concatenate(split(rows), axis=1), tile)
+    return out[:, :w] + out[:, w:]
+
+
+def inv_tiles(c):
+    high, mid, low = split3(c)
+    pair = jnp.concatenate([high, mid], axis=1)
+    return jnp.concatenate([pair, pair], axis=0), jnp.concatenate([low, high], axis=0)
+
+
+def mm_six(rows, tiles):
+    w = rows.shape[1]
+    high, mid, low = split3(rows)
+    one = dot(jnp.concatenate([high, mid], axis=1), tiles[0])
+    two = dot(jnp.concatenate([high, low], axis=1), tiles[1])
+    return (two + one[:, w:]) + one[:, :w]
+
+
+def stencil(pad, x, by, zero):
+    q = pad[x + 1, 1 : by + 1]
+    near = pad[x, 1 : by + 1] + pad[x + 2, 1 : by + 1]
+    near = near + pad[x + 1, 0:by] + pad[x + 1, 2 : by + 2]
+    near = near + jnp.concatenate([q[:, 1:], zero], axis=1)
+    near = near + jnp.concatenate([zero, q[:, :-1]], axis=1)
+    return q, near
+
+
+def field(cells, f, dx, by, bz, w):
+    part = cells[f * bz : (f + 1) * bz]
+    return jnp.stack([jnp.broadcast_to(part[:, dx * by + y : dx * by + y + 1], (bz, w)) for y in range(by)])
 
 
 def factorize(work, upper, inverse):
@@ -56,7 +126,7 @@
         inverse[pl.ds(first, BLK), :] = e
         beyond = jnp.where(lane >= first + BLK, u, 0.0)
         panel = (lane_all >= first) & (lane_all < first + BLK)
-        work[...] = jnp.where(panel, 0.0, work[...]) - mm_t(beyond, beyond + e)
+        work[...] = jnp.where(panel, 0.0, work[...]) - rank_update(beyond, beyond + e)
         return carry
 
     lax.fori_loop(0, n // BLK, block, 0)
@@ -64,10 +134,10 @@
 
 def kernel(
     sizes,
-    y_ref, fields_ref, ritz_ref, shifts_ref,
-    vec_ref, res_ref, stiff_ref, damp_ref, mass_ref, factor_ref,
-    pad, halo_x, halo_y, work, upper, inv_a, inv_b,
-    g_src, g_recv, g_z, g_full, h_recv, h_z, h_full, p_src, p_recv, p_z, p_full, h_src, proj,
+    y_hbm, stiff_in, damp_in, dens_in, ritz_ref,
+    pad, cells_ref, proj, inv_b, factor_ref,
+    y_ref, halo_x, halo_y, work, upper, inv_a,
+    g_src, g_recv, g_z, g_full, h_recv, h_z, h_full, p_src, p_recv, p_z, p_full, h_src, load_sem,
     halo_send, halo_got, a_send, a_got, z_send, z_got, b_send, b_got,
 ):
     nx, ny, nz, all_cells = sizes
@@ -91,6 +161,15 @@
     ]
     peers = [lax.rem(mine + d, group) for d in range(1, group)]
     planes = [lax.rem(iy + d, ny) for d in range(1, ny)]
+
+    parts = 4
+    px = bx // parts
+    loads = [
+        pltpu.make_async_copy(y_hbm.at[pl.ds(i * px, px)], y_ref.at[pl.ds(i * px, px)], load_sem.at[i])
+        for i in range(parts)
+    ]
+    for load in loads:
+        load.start()
 
     barrier = pltpu.get_barrier_semaphore()
     for peer in peers:
@@ -102,11 +181,15 @@
         def _():
             pl.semaphore_signal(barrier, inc=1, device_id=device, device_id_type=MESH)
 
-    def gram_step(i, total):
-        rows = y_ref[pl.ds(i * 4, 4)].reshape(4 * by * bz, w)
-        return total + mm_t(rows, rows)
-
-    work[...] = lax.fori_loop(0, bx // 4, gram_step, jnp.zeros((w, w), F32))
+    total = jnp.zeros((w, w), F32)
+    for i in range(parts):
+        loads[i].wait()
+        rows = y_ref[i * px : (i + 1) * px].reshape(px * by * bz, w)
+        total = total + mm_t(rows, rows)
+    work[...] = total
+
+    empty = jnp.zeros((bx * by, w - 3 * bz), F32)
+    cells_ref[...] = jnp.concatenate([stiff_in[...], damp_in[...], dens_in[...], empty], axis=1).T
 
     beside = sum(exists.astype(jnp.int32) for exists, _, _, _, _ in sides)
     pl.semaphore_wait(barrier, group - 1 + ny - 1 + beside)
@@ -197,107 +280,117 @@
         def _():
             halo_copy(k).wait_send()
             halo_copy(k ^ 1).wait_recv()
-    first_inv = inv_a[...].T
+    tiles = inv_tiles(inv_a[...].T)
 
     def basis_step(i, carry):
         rows = y_ref[pl.ds(i * 4, 4)].reshape(4 * by * bz, w)
-        pad[pl.ds(i * 4 + 1, 4), 1 : by + 1] = mm(rows, first_inv).reshape(4, by, bz, w)
+        pad[pl.ds(i * 4 + 1, 4), 1 : by + 1] = mm_six(rows, tiles).reshape(4, by, bz, w)
         return carry
-
-    lax.fori_loop(0, bx // 4, basis_step, 0)
-    for side, at in ((0, 0), (1, bx + 1)):
-        pad[at, 1 : by + 1] = mm(halo_x[side].reshape(by * bz, w), first_inv).reshape(by, bz, w)
-    for side, at in ((0, 0), (1, by + 1)):
-        pad[1 : bx + 1, at] = mm(halo_y[side].reshape(bx * bz, w), first_inv).reshape(bx, bz, w)
-
-    zero = jnp.zeros((by, 1, w), F32)
-
-    def near_of(x):
-        q = pad[x + 1, 1 : by + 1]
-        near = pad[x, 1 : by + 1] + pad[x + 2, 1 : by + 1]
-        near = near + pad[x + 1, 0:by] + pad[x + 1, 2 : by + 2]
-        near = near + jnp.concatenate([q[:, 1:], zero], axis=1)
-        near = near + jnp.concatenate([zero, q[:, :-1]], axis=1)
-        return q, near
-
-    def field(f, x):
-        cell = fields_ref[f, x]
-        return jnp.stack([jnp.broadcast_to(cell[:, y : y + 1], (bz, w)) for y in range(by)])
-
-    def flat(v):
-        return v.reshape(by * bz, w)
 
     def gram_two_step(i, total):
         rows = pad[pl.ds(i * 4 + 1, 4), 1 : by + 1].reshape(4 * by * bz, w)
-        return total + mm_t(rows, rows)
-
-    h = lax.fori_loop(0, bx // 4, gram_two_step, jnp.zeros((w, w), F32))
-    work[...] = h
+        high, low = split(rows)
+        return total + dot_t(high, jnp.concatenate([high, low], axis=1))
+
+    lax.fori_loop(0, bx // 4, basis_step, 0)
+    pair = lax.fori_loop(0, bx // 4, gram_two_step, jnp.zeros((w, 2 * w), F32))
+    cross = pair[:, w:]
+    work[...] = pair[:, :w] + (cross + cross.T)
     chunks(work, h_src)
     t1 = scatter_start(1, h_src, h_recv)
 
+    for side, at in ((0, 0), (1, bx + 1)):
+        pad[at, 1 : by + 1] = mm_six(halo_x[side].reshape(by * bz, w), tiles).reshape(by, bz, w)
+    for side, at in ((0, 0), (1, by + 1)):
+        pad[1 : bx + 1, at] = mm_six(halo_y[side].reshape(bx * bz, w), tiles).reshape(bx, bz, w)
+    for at_x in (0, bx + 1):
+        for at_y in (0, by + 1):
+            pad[at_x, at_y] = jnp.zeros((bz, w), F32)
+
+    zero = jnp.zeros((by, 1, w), F32)
+    lanes = bx * by
     proj[...] = jnp.zeros(proj.shape, F32)
 
-    def proj_step(x, carry):
-        q, near = near_of(x)
-        k_block = (6.0 + field(0, x)) * q - near
-        c_block = field(1, x) * q
-        m_block = field(2, x) * q + near * (1.0 / 12.0)
-        wide = jnp.concatenate([flat(k_block), flat(c_block), flat(m_block)], axis=1)
-        out = mm_t(flat(q), wide)
+    def proj_step(i, carry):
+        cells = pltpu.roll(cells_ref[0 : 3 * bz, :], lax.rem(lanes - i * 2 * by, lanes), 1)
+        qs, wides = [], []
+        for dx in range(2):
+            q, near = stencil(pad, i * 2 + dx, by, zero)
+            k_block = (6.0 + field(cells, 0, dx, by, bz, w)) * q - near
+            c_block = field(cells, 1, dx, by, bz, w) * q
+            m_block = field(cells, 2, dx, by, bz, w) * q + near * (1.0 / 12.0)
+            qs.append(q.reshape(by * bz, w))
+            wides.append(jnp.concatenate([v.reshape(by * bz, w) for v in (k_block, c_block, m_block)], axis=1))
+        qh, ql = split(jnp.concatenate(qs, axis=0))
+        vh, vl = split(jnp.concatenate(wides, axis=0))
+        out = dot_t(ql, vh) + dot_t(qh, vl) + dot_t(qh, vh)
         for p in range(3):
             proj[p * w : (p + 1) * w, :] += out[:, p * w : (p + 1) * w]
         return carry
 
-    lax.fori_loop(0, bx, proj_step, 0)
+    third = bx // 2 // 3
+    lax.fori_loop(0, third, proj_step, 0)
+    t2 = plane_start(1, t1, h_src, h_recv, h_z)
+    lax.fori_loop(third, 2 * third, proj_step, 0)
+    t3 = gather_start(1, t2, h_z, h_full)
+    lax.fori_loop(2 * third, bx // 2, proj_step, 0)
     chunks(proj, p_src)
     r1 = scatter_start(2, p_src, p_recv)
-    t2 = plane_start(1, t1, h_src, h_recv, h_z)
-    t3 = gather_start(1, t2, h_z, h_full)
-    r2 = plane_start(2, r1, p_src, p_recv, p_z)
     gather_end(t3, h_full, work)
     factorize(work, upper, inv_b)
-    r3 = gather_start(2, r2, p_z, p_full)
-
-    left = inv_b[...]
-    second_inv = left.T
-    coeffs = mm(second_inv, ritz_ref[...])
+    r2 = plane_start(2, r1, p_src, p_recv, p_z)
+    tile = coeff_tile(mm(inv_b[...].T, ritz_ref[...]))
 
     def vector_step(i, carry):
         rows = pad[pl.ds(i * 2, 2)].reshape(2 * (by + 2) * bz, w)
-        pad[pl.ds(i * 2, 2)] = mm(rows, coeffs).reshape(2, by + 2, bz, w)
+        pad[pl.ds(i * 2, 2)] = mm_three(rows, tile).reshape(2, by + 2, bz, w)
         return carry
 
-    pad[0, 0] = jnp.zeros((bz, w), F32)
-    pad[0, by + 1] = jnp.zeros((bz, w), F32)
-    pad[bx + 1, 0] = jnp.zeros((bz, w), F32)
-    pad[bx + 1, by + 1] = jnp.zeros((bz, w), F32)
     lax.fori_loop(0, (bx + 2) // 2, vector_step, 0)
+    r3 = gather_start(2, r2, p_z, p_full)
+    for copies in (s1, s2, s3, t1, t2, t3, r1, r2):
+        for copy in copies:
+            copy.wait_send()
+    gather_end(r3, p_full, proj)
+    for copy in r3:
+        copy.wait_send()
+
+
+def finish(
+    pad, cells_ref, proj, inv_ref, factor_in, shifts_ref,
+    vec_ref, res_ref, stiff_ref, damp_ref, mass_ref, factor_ref,
+):
+    step = pl.program_id(0)
+    px, by, bz, w = vec_ref.shape
+    lanes = cells_ref.shape[1]
+    zero = jnp.zeros((by, 1, w), F32)
+    cells = pltpu.roll(cells_ref[0 : 3 * bz, :], lax.rem(lanes - step * px * by, lanes), 1)
     shifts = shifts_ref[...].reshape(1, 1, w)
     squares = shifts * shifts
-
-    def residual_step(x, carry):
-        v, near = near_of(x)
-        vec_ref[x] = v
-        stiff = (6.0 + field(0, x)) * v - near
-        res_ref[x] = stiff + field(1, x) * v * shifts + (field(2, x) * v + near * (1.0 / 12.0)) * squares
-        return carry
-
-    lax.fori_loop(0, bx, residual_step, 0)
-
-    gather_end(r3, p_full, proj)
-    for p, out in enumerate((stiff_ref, damp_ref, mass_ref)):
-        out[...] = mm(left, mm(proj[p * w : (p + 1) * w, :], second_inv))
-    for copies in (s1, s2, s3, t1, t2, t3, r1, r2, r3):
-        for copy in copies:
-            copy.wait_send()
+    near_scale = squares * (1.0 / 12.0) - 1.0
+    for dx in range(px):
+        v, near = stencil(pad, step * px + dx, by, zero)
+        vec_ref[dx] = v
+        diag = (6.0 + field(cells, 0, dx, by, bz, w)) + field(cells, 1, dx, by, bz, w) * shifts
+        diag = diag + field(cells, 2, dx, by, bz, w) * squares
+        res_ref[dx] = diag * v + near_scale * near
+
+    @pl.when(step == 0)
+    def _():
+        left = inv_ref[...]
+        mid = mm(proj[...], left.T)
+        out = mm(left, jnp.concatenate([mid[p * w : (p + 1) * w] for p in range(3)], axis=1))
+        stiff_ref[...] = out[:, :w]
+        damp_ref[...] = out[:, w : 2 * w]
+        mass_ref[...] = out[:, 2 * w :]
+        factor_ref[...] = factor_in[...]
 
 
 def local(sizes, moments, stiffness, damping, density, ritz_coeffs, shifts):
     nx, ny, nz, _ = sizes
     bx, by, bz, w = moments.shape
     group = nx * nz
-    fields = jnp.stack([stiffness, damping, density]).transpose(0, 1, 3, 2)
+    flat = [f.reshape(bx * by, bz) for f in (stiffness, damping, density)]
     r = w // group
     q = 3 * w // group
     mat = jax.ShapeDtypeStruct((w, w), F32)
@@ -305,16 +398,19 @@
     square = pltpu.VMEM((w, w), F32)
     vmem = pl.BlockSpec(memory_space=pltpu.VMEM)
     dma = pltpu.SemaphoreType.DMA
-    return pl.pallas_call(
+    padded = (bx + 2, by + 2, bz, w)
+    shared = pl.pallas_call(
         functools.partial(kernel, sizes),
-        out_shape=(block, block, mat, mat, mat, mat),
-        in_specs=[vmem] * 4,
-        out_specs=(vmem,) * 6,
+        out_shape=(
+            jax.ShapeDtypeStruct(padded, F32), mat, jax.ShapeDtypeStruct((3 * w, w), F32), mat, mat,
+        ),
+        in_specs=[pl.BlockSpec(memory_space=pl.ANY)] + [vmem] * 4,
+        out_specs=(vmem,) * 5,
         scratch_shapes=[
-            pltpu.VMEM((bx + 2, by + 2, bz, w), F32),
+            pltpu.VMEM(moments.shape, F32),
             pltpu.VMEM((2, by, bz, w), F32),
             pltpu.VMEM((2, bx, bz, w), F32),
-            square, square, square, square,
+            square, square, square,
             pltpu.VMEM((group, r, w), F32),
             pltpu.VMEM((group, r, w), F32),
             pltpu.VMEM((ny, r, w), F32),
@@ -327,16 +423,27 @@
             pltpu.VMEM((ny, q, w), F32),
             pltpu.VMEM((group, q, w), F32),
             pltpu.VMEM((group, r, w), F32),
-            pltpu.VMEM((3 * w, w), F32),
+            dma((4,)),
             dma((4,)), dma((4,)),
             dma((3, group - 1)), dma((3, group - 1)),
             dma((3, ny - 1)), dma((3, ny - 1)),
             dma((3, group - 1)), dma((3, group - 1)),
         ],
         compiler_params=pltpu.CompilerParams(
-            collective_id=0, has_side_effects=True, vmem_limit_bytes=48 << 20
+            collective_id=0, has_side_effects=True, vmem_limit_bytes=24 << 20
         ),
-    )(moments, fields, ritz_coeffs, shifts.reshape(1, w))
+    )(moments, *flat, ritz_coeffs)
+    px = 4
+    tile = pl.BlockSpec((px, by, bz, w), lambda i: (i, 0, 0, 0))
+    whole = pl.BlockSpec((w, w), lambda i: (0, 0))
+    return pl.pallas_call(
+        finish,
+        grid=(bx // px,),
+        out_shape=(block, block, mat, mat, mat, mat),
+        in_specs=[vmem] * 6,
+        out_specs=(tile, tile, whole, whole, whole, whole),
+        compiler_params=pltpu.CompilerParams(vmem_limit_bytes=24 << 20),
+    )(*shared, shifts.reshape(1, w))
 
 
 def solution(mesh):

time: 64.5 us -> 54.8 us (0.85)
  Pallas kernels: 55.3 us -> 48.5 us
  local copies, waits for them, and re-layouts: 8.12 us -> 5.22 us
    pallas_call x1 -> x2, Pallas kernels: 55.3 us -> 48.5 us  [the longest x1 44.6 us: local(): pl.pallas_call(functools.partial(kernel, sizes), out_shape=(jax.ShapeDtyp...]
    unnamed x15 -> x12, local copies, waits for them, and re-layouts: 8.12 us -> 5.22 us
where the time goes in v2:
time: 54.8 us; the launch traced here: 54.4 us
  Pallas kernels  48.5 us (89%)
  local copies, waits for them, and re-layouts  5.22 us (10%)
  between operations  0.66 us (1%)
    pallas_call x1, Pallas kernels, local(): pl.pallas_call(functools.partial(kernel, sizes), out_shape=(jax.ShapeDtyp...  44.6 us
    unnamed x12, local copies, waits for them, and re-layouts  5.22 us
    pallas_call x1, Pallas kernels, local(): pl.pallas_call(finish, grid=(bx // px,), out_shape=(block, block, mat, ma...  3.93 us

profile of v2, /device:TPU:0, one launch (start us, length us, event | category | flops | bytes accessed | tf_op | source)
XLA Modules:
  0.0 54.4 jit_solution(6164906582623427540)
XLA Ops:
  0.6 0.0 copy-start
  0.6 1.2 %copy-done = f32[16,8,16,128]{3,2,1,0:T(8,128)S(1)} copy-done((f32[16,8,16,128]{3,2,1,0:T(8,128)S(1)}, f32[16,8,16,128]{3,2,1,0:T(8,128)}, u32[]{:S(2)}) %copy-start) | copy-done | bytes 1048600
  1.9 0.0 copy-start.1
  1.9 0.8 %copy-done.1 = f32[16,8,16]{2,1,0:T(8,128)S(1)} copy-done((f32[16,8,16]{2,1,0:T(8,128)S(1)}, f32[16,8,16]{2,1,0:T(8,128)}, u32[]{:S(2)}) %copy-start.1) | copy-done | bytes 8216
  2.7 0.0 copy-start.2
  2.7 0.8 %copy-done.2 = f32[16,8,16]{2,1,0:T(8,128)S(1)} copy-done((f32[16,8,16]{2,1,0:T(8,128)S(1)}, f32[16,8,16]{2,1,0:T(8,128)}, u32[]{:S(2)}) %copy-start.2) | copy-done | bytes 8216
  3.5 0.0 copy-start.3
  3.5 0.8 %copy-done.3 = f32[16,8,16]{2,1,0:T(8,128)S(1)} copy-done((f32[16,8,16]{2,1,0:T(8,128)S(1)}, f32[16,8,16]{2,1,0:T(8,128)}, u32[]{:S(2)}) %copy-start.3) | copy-done | bytes 8216
  4.4 0.0 copy-start.4
  4.4 0.8 %copy-done.4 = f32[128,128]{1,0:T(8,128)S(1)} copy-done((f32[128,128]{1,0:T(8,128)S(1)}, f32[128,128]{1,0:T(8,128)}, u32[]{:S(2)}) %copy-start.4) | copy-done | bytes 65560
  5.2 44.6 %shard_map.109 = (f32[18,10,16,128]{3,2,1,0:T(8,128)S(1)}, f32[128,128]{1,0:T(8,128)S(1)}, f32[384,128]{1,0:T(8,128)S(1)}, f32[128,128]{1,0:T(8,128)S(1)}, f32[128,128]{1,0:T(8,128)S(1)}) custom-call(f32[16,8,16,128]{3,2,1,0:T(8,128)S(1)} %copy-done, f32[128,16]{1,0:T(8,128)S(1)} %bitcast.4, f32[128,16]{1,0:T(8,128)S(1)} %bitcast.5, f32[128,16]{1,0:T(8,128)S(1)} %bitcast.6, ...), custom_call_target="tpu_custom_call" | custom-call | tf_op jit(solution)/shard_map/pallas_call | solution.py:402
  49.8 0.0 copy-start.5
  49.8 0.6 %copy-done.5 = f32[128]{0:T(128)S(1)} copy-done((f32[128]{0:T(128)S(1)}, f32[128]{0:T(128)}, u32[]{:S(2)}) %copy-start.5) | copy-done | bytes 536
  50.5 3.9 %shard_map.110 = (f32[16,8,16,128]{3,2,1,0:T(8,128)}, f32[16,8,16,128]{3,2,1,0:T(8,128)}, f32[128,128]{1,0:T(8,128)}, f32[128,128]{1,0:T(8,128)}, f32[128,128]{1,0:T(8,128)}, /*index=5*/f32[128,128]{1,0:T(8,128)}) custom-call(f32[18,10,16,128]{3,2,1,0:T(8,128)S(1)} %get-tuple-element.11.pad, f32[128,128]{1,0:T(8,128)S(1)} %get-tuple-element.12.cells_ref, ...), custom_call_target="tpu_custom_call" | custom-call | tf_op jit(solution)/shard_map/pallas_call | solution.py:439
Async XLA Ops:
  0.6 1.2 %copy-start = (f32[16,8,16,128]{3,2,1,0:T(8,128)S(1)}, f32[16,8,16,128]{3,2,1,0:T(8,128)}, u32[]{:S(2)}) copy-start(f32[16,8,16,128]{3,2,1,0:T(8,128)} %y_hbm.1) | copy-start | bytes 3145732
  1.9 0.8 %copy-start.1 = (f32[16,8,16]{2,1,0:T(8,128)S(1)}, f32[16,8,16]{2,1,0:T(8,128)}, u32[]{:S(2)}) copy-start(f32[16,8,16]{2,1,0:T(8,128)} %param.7) | copy-start | bytes 24580
  2.7 0.8 %copy-start.2 = (f32[16,8,16]{2,1,0:T(8,128)S(1)}, f32[16,8,16]{2,1,0:T(8,128)}, u32[]{:S(2)}) copy-start(f32[16,8,16]{2,1,0:T(8,128)} %param.8) | copy-start | bytes 24580
  3.5 0.8 %copy-start.3 = (f32[16,8,16]{2,1,0:T(8,128)S(1)}, f32[16,8,16]{2,1,0:T(8,128)}, u32[]{:S(2)}) copy-start(f32[16,8,16]{2,1,0:T(8,128)} %param.9) | copy-start | bytes 24580
  4.4 0.8 %copy-start.4 = (f32[128,128]{1,0:T(8,128)S(1)}, f32[128,128]{1,0:T(8,128)}, u32[]{:S(2)}) copy-start(f32[128,128]{1,0:T(8,128)} %ritz_ref.1) | copy-start | bytes 196612
  49.8 0.7 %copy-start.5 = (f32[128]{0:T(128)S(1)}, f32[128]{0:T(128)}, u32[]{:S(2)}) copy-start(f32[128]{0:T(128)} %param.11) | copy-start | bytes 1540

commit v3 on v2

--- a/solution.py
+++ b/solution.py
@@ -91,7 +91,7 @@
     return jnp.stack([jnp.broadcast_to(part[:, dx * by + y : dx * by + y + 1], (bz, w)) for y in range(by)])
 
 
-def factorize(work, upper, inverse):
+def factorize(work, upper, inverse, between=None):
     n = work.shape[0]
     lane = lax.broadcasted_iota(jnp.int32, (BLK, n), 1)
     sub = lax.broadcasted_iota(jnp.int32, (BLK, n), 0)
@@ -129,22 +129,28 @@
         work[...] = jnp.where(panel, 0.0, work[...]) - rank_update(beyond, beyond + e)
         return carry
 
-    lax.fori_loop(0, n // BLK, block, 0)
+    late = n // BLK * 3 // 4
+    lax.fori_loop(0, late, block, 0)
+    result = between() if between else None
+    lax.fori_loop(late, n // BLK, block, 0)
+    return result
 
 
 def kernel(
     sizes,
-    y_hbm, stiff_in, damp_in, dens_in, ritz_ref,
-    pad, cells_ref, proj, inv_b, factor_ref,
-    y_ref, halo_x, halo_y, work, upper, inv_a,
+    y_hbm, stiff_in, damp_in, dens_in, ritz_in,
+    pad_out, cells_out, proj_out, inv_out, factor_out,
+    pad, cells_ref, proj, inv_b, factor_ref, out_sem,
+    y_ref, fields, ritz_ref, halo_x, halo_y, work, upper, inv_a,
     g_src, g_recv, g_z, g_full, h_recv, h_z, h_full, p_src, p_recv, p_z, p_full, h_src, load_sem,
     halo_send, halo_got, a_send, a_got, z_send, z_got, b_send, b_got,
 ):
     nx, ny, nz, all_cells = sizes
     bx, by, bz, w = y_ref.shape
-    group = nx * nz
+    group, levels = g_recv.shape[0], g_z.shape[0]
     ix, iy, iz = lax.axis_index("gx"), lax.axis_index("gy"), lax.axis_index("gz")
     mine = ix * nz + iz
+    level = iy
     line = iy * nz + iz
 
     def group_id(a):
@@ -160,7 +166,7 @@
         (line < ny * nz - 1, line_id(line + 1), y_ref.at[:, by - 1], halo_y.at[0], halo_y.at[1]),
     ]
     peers = [lax.rem(mine + d, group) for d in range(1, group)]
-    planes = [lax.rem(iy + d, ny) for d in range(1, ny)]
+    planes = [lax.rem(iy + d, ny) for d in range(1, levels)]
 
     parts = 4
     px = bx // parts
@@ -168,6 +174,9 @@
         pltpu.make_async_copy(y_hbm.at[pl.ds(i * px, px)], y_ref.at[pl.ds(i * px, px)], load_sem.at[i])
         for i in range(parts)
     ]
+    for f, src in enumerate((stiff_in, damp_in, dens_in)):
+        loads.append(pltpu.make_async_copy(src, fields.at[f], load_sem.at[parts + f]))
+    loads.append(pltpu.make_async_copy(ritz_in, ritz_ref, load_sem.at[parts + 3]))
     for load in loads:
         load.start()
 
@@ -189,10 +198,19 @@
     work[...] = total
 
     empty = jnp.zeros((bx * by, w - 3 * bz), F32)
-    cells_ref[...] = jnp.concatenate([stiff_in[...], damp_in[...], dens_in[...], empty], axis=1).T
+    for load in loads[parts:]:
+        load.wait()
+    cells_ref[...] = jnp.concatenate([fields[0], fields[1], fields[2], empty], axis=1).T
+    stores = [
+        pltpu.make_async_copy(a, b, out_sem.at[i])
+        for i, (a, b) in enumerate((
+            (cells_ref, cells_out), (factor_ref, factor_out), (inv_b, inv_out), (pad, pad_out), (proj, proj_out),
+        ))
+    ]
+    stores[0].start()
 
     beside = sum(exists.astype(jnp.int32) for exists, _, _, _, _ in sides)
-    pl.semaphore_wait(barrier, group - 1 + ny - 1 + beside)
+    pl.semaphore_wait(barrier, group - 1 + levels - 1 + beside)
 
     def halo_copy(k):
         _, device, src, dst, _ = sides[k]
@@ -219,11 +237,11 @@
         total = src[mine]
         for d in range(group - 1):
             total = total + recv[d]
-        z[iy] = total
+        z[level] = total
         after = []
         for d, plane in enumerate(planes):
             copy = pltpu.make_async_remote_copy(
-                src_ref=z.at[iy], dst_ref=z.at[iy], send_sem=z_send.at[slot, d],
+                src_ref=z.at[level], dst_ref=z.at[level], send_sem=z_send.at[slot, d],
                 recv_sem=z_got.at[slot, d], device_id=(ix, plane, iz), device_id_type=MESH,
             )
             copy.start()
@@ -234,7 +252,7 @@
         for copy in copies:
             copy.wait_recv()
         total = z[0]
-        for d in range(1, ny):
+        for d in range(1, levels):
             total = total + z[d]
         full[mine] = total
         after = []
@@ -261,6 +279,9 @@
 
     chunks(work, g_src)
     s1 = scatter_start(0, g_src, g_recv)
+    s2 = plane_start(0, s1, g_src, g_recv, g_z)
+    s3 = gather_start(0, s2, g_z, g_full)
+    gather_end(s3, g_full, work)
     for k, (exists, _, _, _, land) in enumerate(sides):
         @pl.when(exists)
         def _():
@@ -269,11 +290,9 @@
         @pl.when(jnp.logical_not(exists))
         def _():
             land[...] = jnp.zeros(land.shape, F32)
-    s2 = plane_start(0, s1, g_src, g_recv, g_z)
-    s3 = gather_start(0, s2, g_z, g_full)
-    gather_end(s3, g_full, work)
     factorize(work, upper, inv_a)
     factor_ref[...] = upper[...] / math.sqrt(all_cells)
+    stores[1].start()
 
     for k, (exists, _, _, _, _) in enumerate(sides):
         @pl.when(exists)
@@ -337,8 +356,9 @@
     chunks(proj, p_src)
     r1 = scatter_start(2, p_src, p_recv)
     gather_end(t3, h_full, work)
-    factorize(work, upper, inv_b)
-    r2 = plane_start(2, r1, p_src, p_recv, p_z)
+    r2 = factorize(work, upper, inv_b, lambda: plane_start(2, r1, p_src, p_recv, p_z))
+    stores[2].start()
+    r3 = gather_start(2, r2, p_z, p_full)
     tile = coeff_tile(mm(inv_b[...].T, ritz_ref[...]))
 
     def vector_step(i, carry):
@@ -347,20 +367,39 @@
         return carry
 
     lax.fori_loop(0, (bx + 2) // 2, vector_step, 0)
-    r3 = gather_start(2, r2, p_z, p_full)
+    stores[3].start()
     for copies in (s1, s2, s3, t1, t2, t3, r1, r2):
         for copy in copies:
             copy.wait_send()
     gather_end(r3, p_full, proj)
+    stores[4].start()
     for copy in r3:
         copy.wait_send()
+    for store in stores:
+        store.wait()
 
 
 def finish(
-    pad, cells_ref, proj, inv_ref, factor_in, shifts_ref,
+    pad_in, cells_in, proj_in, inv_in, factor_in, shifts_in,
     vec_ref, res_ref, stiff_ref, damp_ref, mass_ref, factor_ref,
+    pad, cells_ref, proj, inv_ref, shifts_ref, sems,
 ):
     step = pl.program_id(0)
+
+    def loads():
+        pairs = (
+            (cells_in, cells_ref), (shifts_in, shifts_ref), (pad_in, pad),
+            (proj_in, proj), (inv_in, inv_ref), (factor_in, factor_ref),
+        )
+        return [pltpu.make_async_copy(a, b, sems.at[i]) for i, (a, b) in enumerate(pairs)]
+
+    @pl.when(step == 0)
+    def _():
+        for load in loads():
+            load.start()
+        for load in loads():
+            load.wait()
+
     px, by, bz, w = vec_ref.shape
     lanes = cells_ref.shape[1]
     zero = jnp.zeros((by, 1, w), F32)
@@ -383,20 +422,19 @@
         stiff_ref[...] = out[:, :w]
         damp_ref[...] = out[:, w : 2 * w]
         mass_ref[...] = out[:, 2 * w :]
-        factor_ref[...] = factor_in[...]
 
 
 def local(sizes, moments, stiffness, damping, density, ritz_coeffs, shifts):
     nx, ny, nz, _ = sizes
     bx, by, bz, w = moments.shape
-    group = nx * nz
+    group, levels = nx * nz, ny
     flat = [f.reshape(bx * by, bz) for f in (stiffness, damping, density)]
     r = w // group
     q = 3 * w // group
     mat = jax.ShapeDtypeStruct((w, w), F32)
     block = jax.ShapeDtypeStruct(moments.shape, F32)
     square = pltpu.VMEM((w, w), F32)
-    vmem = pl.BlockSpec(memory_space=pltpu.VMEM)
+    hbm = pl.BlockSpec(memory_space=pltpu.HBM)
     dma = pltpu.SemaphoreType.DMA
     padded = (bx + 2, by + 2, bz, w)
     shared = pl.pallas_call(
@@ -404,33 +442,40 @@
         out_shape=(
             jax.ShapeDtypeStruct(padded, F32), mat, jax.ShapeDtypeStruct((3 * w, w), F32), mat, mat,
         ),
-        in_specs=[pl.BlockSpec(memory_space=pl.ANY)] + [vmem] * 4,
-        out_specs=(vmem,) * 5,
+        in_specs=[hbm] * 5,
+        out_specs=(hbm,) * 5,
         scratch_shapes=[
+            pltpu.VMEM(padded, F32),
+            square,
+            pltpu.VMEM((3 * w, w), F32),
+            square, square,
+            dma((5,)),
             pltpu.VMEM(moments.shape, F32),
+            pltpu.VMEM((3, bx * by, bz), F32),
+            pltpu.VMEM((w, w), F32),
             pltpu.VMEM((2, by, bz, w), F32),
             pltpu.VMEM((2, bx, bz, w), F32),
             square, square, square,
             pltpu.VMEM((group, r, w), F32),
             pltpu.VMEM((group, r, w), F32),
-            pltpu.VMEM((ny, r, w), F32),
+            pltpu.VMEM((levels, r, w), F32),
             pltpu.VMEM((group, r, w), F32),
             pltpu.VMEM((group, r, w), F32),
-            pltpu.VMEM((ny, r, w), F32),
+            pltpu.VMEM((levels, r, w), F32),
             pltpu.VMEM((group, r, w), F32),
             pltpu.VMEM((group, q, w), F32),
             pltpu.VMEM((group, q, w), F32),
-            pltpu.VMEM((ny, q, w), F32),
+            pltpu.VMEM((levels, q, w), F32),
             pltpu.VMEM((group, q, w), F32),
             pltpu.VMEM((group, r, w), F32),
-            dma((4,)),
+            dma((8,)),
             dma((4,)), dma((4,)),
             dma((3, group - 1)), dma((3, group - 1)),
-            dma((3, ny - 1)), dma((3, ny - 1)),
+            dma((3, max(levels - 1, 1))), dma((3, max(levels - 1, 1))),
             dma((3, group - 1)), dma((3, group - 1)),
         ],
         compiler_params=pltpu.CompilerParams(
-            collective_id=0, has_side_effects=True, vmem_limit_bytes=24 << 20
+            collective_id=0, has_side_effects=True, vmem_limit_bytes=60 << 20
         ),
     )(moments, *flat, ritz_coeffs)
     px = 4
@@ -440,9 +485,12 @@
         finish,
         grid=(bx // px,),
         out_shape=(block, block, mat, mat, mat, mat),
-        in_specs=[vmem] * 6,
+        in_specs=[hbm] * 6,
         out_specs=(tile, tile, whole, whole, whole, whole),
-        compiler_params=pltpu.CompilerParams(vmem_limit_bytes=24 << 20),
+        scratch_shapes=[
+            pltpu.VMEM(padded, F32), square, pltpu.VMEM((3 * w, w), F32), square, pltpu.VMEM((1, w), F32), dma((6,)),
+        ],
+        compiler_params=pltpu.CompilerParams(vmem_limit_bytes=60 << 20),
     )(*shared, shifts.reshape(1, w))
 
 

time: 54.8 us -> 51.5 us (0.940)
  local copies, waits for them, and re-layouts: 5.22 us -> 0 us
  Pallas kernels: 48.5 us -> 50.7 us
    unnamed x12 -> x0, local copies, waits for them, and re-layouts: 5.22 us -> none
    pallas_call x1, Pallas kernels: 3.93 us -> 5.45 us  [local(): pl.pallas_call(finish, grid=(bx // px,), out_shape=(block, block, mat, ma...]
    pallas_call x1, Pallas kernels: 44.6 us -> 45.3 us  [local(): pl.pallas_call(functools.partial(kernel, sizes), out_shape=(jax.ShapeDtyp...]
where the time goes in v3:
time: 51.5 us; the launch traced here: 51.4 us
  Pallas kernels  50.7 us (98%)
  between operations  0.64 us (1%)
    pallas_call x1, Pallas kernels, local(): pl.pallas_call(functools.partial(kernel, sizes), out_shape=(jax.ShapeDtyp...  45.3 us
    pallas_call x1, Pallas kernels, local(): pl.pallas_call(finish, grid=(bx // px,), out_shape=(block, block, mat, ma...  5.45 us

profile of v3, /device:TPU:0, one launch (start us, length us, event | category | flops | bytes accessed | tf_op | source)
XLA Modules:
  0.0 51.4 jit_solution(73006223125234648)
XLA Ops:
  0.6 45.3 %shard_map.109 = (f32[18,10,16,128]{3,2,1,0:T(8,128)}, f32[128,128]{1,0:T(8,128)}, f32[384,128]{1,0:T(8,128)}, f32[128,128]{1,0:T(8,128)}, f32[128,128]{1,0:T(8,128)}) custom-call(f32[16,8,16,128]{3,2,1,0:T(8,128)} %y_hbm.1, f32[128,16]{1,0:T(8,128)} %bitcast.4, f32[128,16]{1,0:T(8,128)} %bitcast.5, f32[128,16]{1,0:T(8,128)} %bitcast.6, f32[128,128]{1,0:T(8,128)} %ritz_in.1), custom_call_target="tpu_custom_call" | custom-call | tf_op jit(solution)/shard_map/pallas_call | solution.py:440
  45.9 5.4 %shard_map.110 = (f32[16,8,16,128]{3,2,1,0:T(8,128)}, f32[16,8,16,128]{3,2,1,0:T(8,128)}, f32[128,128]{1,0:T(8,128)}, f32[128,128]{1,0:T(8,128)}, f32[128,128]{1,0:T(8,128)}, /*index=5*/f32[128,128]{1,0:T(8,128)}) custom-call(f32[18,10,16,128]{3,2,1,0:T(8,128)} %get-tuple-element.11.pad_in, f32[128,128]{1,0:T(8,128)} %get-tuple-element.12.cells_in, ...), custom_call_target="tpu_custom_call" | custom-call | tf_op jit(solution)/shard_map/pallas_call | solution.py:484
